TPU v7x, 32 devices: a whole 2x2x4 slice. The times are simulated.
32 devices in a mesh: mem: 4 (over y, x), reg: 8 (over z, core).
Axes of the slice: x: 2, y: 2, z: 4, core: 2. Of those that a mesh axis runs over, the one named last changes fastest.
Arguments:
- alpha: float32 [32, 16, 32, 128], P('mem', None, 'reg'), may hold values from -6 to 6
- perturbation: bfloat16 [32, 2, 16, 128, 512], P('mem', None, None, 'reg'), may hold values from -6 to 6
- obs_cell: int32 [8192], P('reg'), may hold values from 0 to 131071
- obs_kind: int32 [8192], P('reg'), may hold values from 0 to 3
- obs_value: float32 [8192], P('reg'), may hold values from -6 to 6
- obs_weight: float32 [8192], P('reg'), may hold values from 1 to 4
Outputs:
- obs_gradient: float32 [32, 16, 32, 128], P('mem', None, 'reg')
Inputs may be any that keep to these rules, and one draw needn't show every extreme that they name: `obs_cell`: each entry is level * 16 * 512 + row * 512 + column of a fine cell, the row counted from the first row of the observation's own region. `obs_kind`: 0 zonal wind, 1 meridional wind, 2 relative vorticity, 3 zonal wind advection.
All inputs are finite; a program needn't handle non-finite values.
Results may differ from a plain program's by a relative error of at most 0.0003.
Values sent between devices are 32-bit elements; how exact they have to be, the bound alone decides.
No kernel may reach another device: no remote copies, remote signals or barrier semaphores. Data moves between devices by JAX's collectives and lax.ppermute only.
A program may use at most 64 MiB of HBM per device.

v0:
```python
import math
import jax
import jax.numpy as jnp
from jax import lax
from jax.sharding import PartitionSpec as P

PASSES = 2
diffuse = 0.2
highest = lax.Precision.HIGHEST


def padded_2(value, sides, width):
    for axis, dim in sides:
        devices, length = (lax.axis_size(axis), value.shape[dim])
        up = [(i, (i + 1) % devices) for i in range(devices - 1)]
        down = [(j, i) for i, j in up]
        last = lax.slice_in_dim(value, length - width, length, axis=dim)
        first = lax.slice_in_dim(value, 0, width, axis=dim)
        before = lax.ppermute(last, axis, up)
        after = lax.ppermute(first, axis, down)
        value = jnp.concatenate([before, value, after], axis=dim)
    return value


def from_behind(value, axis, by):
    devices = lax.axis_size(axis)
    pairs = [(i, i + by) for i in range(devices) if 0 <= i + by < devices]
    return lax.ppermute(value, axis, pairs)


def weights(fine_rows, fine_start, coarse_count, coarse_start):
    finer = (jnp.arange(fine_rows) + fine_start).astype(jnp.float32)
    coarser = (jnp.arange(coarse_count) + coarse_start).astype(jnp.float32)
    where_at = (finer[:, None] + 0.5) / 4.0 - 0.5
    return jnp.maximum(0.0, 1.0 - jnp.abs(where_at - coarser[None, :]))


def one_pass(block):
    padded = jnp.pad(block, ((0, 0), (0, 0), (1, 1), (1, 1)))
    beside_all = (
        padded[:, :, 2:, 1:-1]
        + padded[:, :, :-2, 1:-1]
        + padded[:, :, 1:-1, 2:]
        + padded[:, :, 1:-1, :-2]
    )
    return block + diffuse * (beside_all - 4.0 * block)


def slopes(padded):
    along_x = (padded[..., 2:, 1:-1] - padded[..., :-2, 1:-1]) * 0.5
    along_y = (padded[..., 1:-1, 2:] - padded[..., 1:-1, :-2]) * 0.5
    return (along_x, along_y)


def mask_rows(block, first_row, total_rows):
    rows_here = first_row + jnp.arange(block.shape[2])
    keeping = (rows_here >= 0) & (rows_here < total_rows)
    return jnp.where(keeping[None, None, :, None], block, 0.0)


def smooth_rows(block, passes, keep):
    region = lax.axis_index("reg")
    total_rows = block.shape[2] * lax.axis_size("reg")
    extended = padded_2(block, (("reg", 2),), passes + keep)
    first_row = region * block.shape[2] - passes - keep
    for step in range(passes):
        extended = one_pass(extended)[:, :, 1:-1, :]
        first_row = first_row + 1
        extended = mask_rows(extended, first_row, total_rows)
    return extended


def observe(extended, level_first, obs_cell, obs_kind, obs_value, obs_weight, back_rim):
    levels = extended.shape[1]
    rows = extended.shape[2] - 2
    fine_cols = extended.shape[3] - 2
    zonal_x, zonal_y = slopes(extended[0])
    merid_x, _ = slopes(extended[1])
    zonal = extended[0, :, 1:-1, 1:-1]
    merid = extended[1, :, 1:-1, 1:-1]
    fields = jnp.stack([zonal, merid, merid_x - zonal_y, zonal * zonal_x + merid * zonal_y])
    plane = rows * fine_cols
    level = obs_cell // plane
    rest = obs_cell % plane
    row_in = rest // fine_cols
    column = rest % fine_cols
    inside = (level >= level_first) & (level < level_first + levels)
    local_level = jnp.clip(level - level_first, 0, levels - 1)
    line_count = 4 * levels * rows
    line = obs_kind * (levels * rows) + local_level * rows + row_in
    line_hot = (line[:, None] == jnp.arange(line_count, dtype=jnp.int32)[None, :]).astype(
        jnp.float32
    )
    column_hot = (column[:, None] == jnp.arange(fine_cols, dtype=jnp.int32)[None, :]).astype(
        jnp.float32
    )
    table = fields.reshape(line_count, fine_cols)
    picked = jnp.dot(line_hot, table, precision=highest, preferred_element_type=jnp.float32)
    seen = jnp.sum(picked * column_hot, axis=1)
    misfit = jnp.where(inside, obs_weight * (seen - obs_value), 0.0)
    weighted = misfit[:, None] * column_hot
    adjoint = lax.dot_general(
        line_hot,
        weighted,
        (((0,), (0,)), ((), ())),
        precision=highest,
        preferred_element_type=jnp.float32,
    )
    adjoint = adjoint.reshape(4, levels, rows, fine_cols)
    back = back_rim(jnp.stack([adjoint[2], adjoint[3] * zonal, adjoint[3] * merid]))
    vort_x, vort_y = slopes(back[0])
    flux_x, _ = slopes(back[1])
    _, flux_y = slopes(back[2])
    grad_u = adjoint[0] + adjoint[3] * zonal_x + vort_y - flux_x - flux_y
    grad_v = adjoint[1] + adjoint[3] * zonal_y - vort_x
    return jnp.stack([grad_u, grad_v])


def local(alpha, perturbation, obs_cell, obs_kind, obs_value, obs_weight):
    members, levels, coarse_rows, coarse_cols = alpha.shape
    fine_rows = perturbation.shape[3]
    region = lax.axis_index("reg")
    scale = 1.0 / math.sqrt(members * lax.axis_size("mem"))
    rows_x = weights(fine_rows, region * fine_rows, coarse_rows + 2, region * coarse_rows - 1)
    rows_y = weights(perturbation.shape[4], 0, coarse_cols, 0)
    smoothed = smooth_rows(alpha, PASSES, 1)
    part = jnp.einsum("ia,mlab->mlib", rows_x, smoothed, precision=highest)
    fine = jnp.einsum("mlib,jb->mlij", part, rows_y, precision=highest)
    partial_value = jnp.sum(fine[:, None] * perturbation.astype(jnp.float32), axis=0) * scale
    whole = lax.psum(partial_value, "mem")
    level_first = 0
    extended = jnp.pad(padded_2(whole, (("reg", 2),), 1), ((0, 0), (0, 0), (0, 0), (1, 1)))

    def back_rim(carried):
        rimmed_rows = padded_2(carried, (("reg", 2),), 1)
        return jnp.pad(rimmed_rows, ((0, 0), (0, 0), (0, 0), (1, 1)))

    grad_fine = observe(extended, level_first, obs_cell, obs_kind, obs_value, obs_weight, back_rim)
    product = jnp.sum(perturbation.astype(jnp.float32) * grad_fine[None], axis=1)
    projected_part = jnp.einsum("mlij,jb->mlib", product, rows_y, precision=highest)
    coarse = jnp.einsum("ia,mlib->mlab", rows_x, projected_part, precision=highest) * scale
    from_above = from_behind(coarse[:, :, 0], "reg", -1)
    from_below = from_behind(coarse[:, :, -1], "reg", 1)
    inner = coarse[:, :, 1:-1]
    inner = inner.at[:, :, -1].add(from_above)
    inner = inner.at[:, :, 0].add(from_below)
    return smooth_rows(inner, PASSES, 0)


def solution(mesh):
    return jax.shard_map(
        local,
        mesh=mesh,
        in_specs=(
            P("mem", None, "reg", None),
            P("mem", None, None, "reg", None),
            P("reg"),
            P("reg"),
            P("reg"),
            P("reg"),
        ),
        out_specs=P("mem", None, "reg", None),
        check_vma=False,
    )
```

profile of v0, /device:TPU:1, one launch (start us, length us, event | category | flops | bytes accessed | tf_op | source)
XLA Modules:
  0.0 147.5 jit_solution(11208299931560446973)
XLA Ops:
  7.7 4.6 %collective-permute-start = (f32[8,16,3,128]{3,1,0,2:T(8,128)S(1)}, f32[8,16,3,128]{3,1,0,2:T(8,128)S(1)}, u32[]{:S(2)}, u32[]{:S(2)}) collective-permute-start(f32[8,16,3,128]{3,1,0,2:T(8,128)S(1)} %copy.30), channel_id=1, source_target_pairs={{0,1},{1,2},{2,3},{3,4},{4,5},{5,6},{6,7},{8,9},{9,10},{10,11},{11... | collective-permute-start | bytes 589832 | tf_op jit(solution)/shard_map/ppermute | solution.py:19
  12.4 1.9 %collective-permute-start.1 = (f32[8,16,3,128]{3,1,0,2:T(8,128)S(1)}, f32[8,16,3,128]{3,1,0,2:T(8,128)S(1)}, u32[]{:S(2)}, u32[]{:S(2)}) collective-permute-start(f32[8,16,3,128]{3,1,0,2:T(8,128)S(1)} %copy.31), channel_id=1, source_target_pairs={{1,0},{2,1},{3,2},{4,3},{5,4},{6,5},{7,6},{9,8},{10,9},{11,10},{12... | collective-permute-start | bytes 589832 | tf_op jit(solution)/shard_map/ppermute | solution.py:20
  15.0 4.4 %collective-permute-done.1 = f32[8,16,3,128]{3,1,0,2:T(8,128)S(1)} collective-permute-done((f32[8,16,3,128]{3,1,0,2:T(8,128)S(1)}, f32[8,16,3,128]{3,1,0,2:T(8,128)S(1)}, u32[]{:S(2)}, u32[]{:S(2)}) %collective-permute-start.1) | collective-permute-done | bytes 196640 | tf_op jit(solution)/shard_map/ppermute | solution.py:20
  21.8 3.5 %fusion.49 = f32[8,16,16,512]{3,2,1,0:T(8,128)S(1)} fusion(f32[8,16,16,128]{3,2,1,0:T(8,128)S(1)} %convolution_bitcast_fusion, f32[128]{0:T(128)S(1)} %iota_convert_fusion, f32[512]{0:T(512)S(1)} %multiply_add_fusion), kind=kOutput, calls=%fused_computation.114 | convolution fusion | flops 1610874880 | bytes 5245440 | tf_op jit(solution)/shard_map/mlib,jb->mlij/dot_general | solution.py:128
  27.6 52.2 %all-reduce.8.cloned.1.call-done = f32[2,16,16,512]{3,2,1,0:T(8,128)} async-done(((f32[2,16,16,512]{3,2,1,0:T(8,128)}), f32[2,16,16,512]{3,2,1,0:T(8,128)}) %all-reduce.8.cloned.1.call-update) | async-done | bytes 1048592 | tf_op jit(solution)/shard_map/psum | solution.py:130
  79.8 1.3 fusion.87
  81.1 3.8 %collective-permute-start.2 = (f32[2,16,1,512]{3,2,1,0:T(1,128)S(1)}, f32[2,16,1,512]{3,2,1,0:T(1,128)S(1)}, u32[]{:S(2)}, u32[]{:S(2)}) collective-permute-start(f32[2,16,1,512]{3,2,1,0:T(1,128)S(1)} %get-tuple-element.44), channel_id=1, source_target_pairs={{0,1},{1,2},{2,3},{3,4},{4,5},{5,6},{6,7},{8,9},{9,10},{10,11},{11... | collective-permute-start | bytes 196616 | tf_op jit(solution)/shard_map/ppermute | solution.py:19
  85.0 2.1 %collective-permute-start.3 = (f32[2,16,1,512]{3,2,1,0:T(1,128)S(1)}, f32[2,16,1,512]{3,2,1,0:T(1,128)S(1)}, u32[]{:S(2)}, u32[]{:S(2)}) collective-permute-start(f32[2,16,1,512]{3,2,1,0:T(1,128)S(1)} %get-tuple-element.45), channel_id=1, source_target_pairs={{1,0},{2,1},{3,2},{4,3},{5,4},{6,5},{7,6},{9,8},{10,9},{11,10},{12... | collective-permute-start | bytes 196616 | tf_op jit(solution)/shard_map/ppermute | solution.py:20
  87.2 3.4 %collective-permute-done.3 = f32[2,16,1,512]{3,2,1,0:T(1,128)S(1)} collective-permute-done((f32[2,16,1,512]{3,2,1,0:T(1,128)S(1)}, f32[2,16,1,512]{3,2,1,0:T(1,128)S(1)}, u32[]{:S(2)}, u32[]{:S(2)}) %collective-permute-start.3) | collective-permute-done | bytes 65568 | tf_op jit(solution)/shard_map/ppermute | solution.py:20
  90.6 2.3 %select_maximum_fusion.4 = f32[2,16,18,514]{3,2,1,0:T(8,128)S(1)} fusion(f32[2,16,1,512]{3,2,1,0:T(1,128)S(1)} %collective-permute-done.3, f32[2,16,16,512]{3,2,1,0:T(8,128)} %all-reduce.8.cloned.1.call-done, f32[2,16,1,512]{3,2,1,0:T(1,128)S(1)} %collective-permute-done.2), kind=kLoop, calls=%fused_computation.34 | loop fusion | flops 2368512 | bytes 2363904 | tf_op jit(solution)/shard_map/concatenate | solution.py:21
  95.2 3.7 %select_reduce_fusion = f32[1024]{0:T(1024)S(1)} fusion(f32[1024,512]{1,0:T(8,128)S(1)} %bitcast.71, s32[1024]{0:T(1024)S(1)} %get-tuple-element.72, s32[1024]{0:T(1024)S(1)} %get-tuple-element.71), kind=kOutput, calls=%fused_computation.30 | convolution fusion | flops 6445071360 | bytes 2109440 | tf_op jit(solution)/shard_map/dot_general | solution.py:98
  98.8 4.2 %fusion.2 = f32[1024,512]{1,0:T(8,128)S(1)} fusion(s32[1024]{0:T(1024)S(1)} %get-tuple-element.72, f32[1024]{0:T(1024)S(1)} %multiply_select_fusion, s32[1024]{0:T(1024)S(1)} %get-tuple-element.71), kind=kOutput, calls=%fused_computation.7 | convolution fusion | flops 6444548096 | bytes 2109440 | tf_op jit(solution)/shard_map/dot_general | solution.py:102
  103.7 1.9 %collective-permute-start.4 = (f32[3,16,1,512]{3,2,1,0:T(1,128)S(1)}, f32[3,16,1,512]{3,2,1,0:T(1,128)S(1)}, u32[]{:S(2)}, u32[]{:S(2)}) collective-permute-start(f32[3,16,1,512]{3,2,1,0:T(1,128)S(1)} %get-tuple-element.40), channel_id=1, source_target_pairs={{0,1},{1,2},{2,3},{3,4},{4,5},{5,6},{6,7},{8,9},{9,10},{10,11},{11... | collective-permute-start | bytes 294920 | tf_op jit(solution)/shard_map/ppermute | solution.py:19
  105.6 2.6 %collective-permute-start.5 = (f32[3,16,1,512]{3,2,1,0:T(1,128)S(1)}, f32[3,16,1,512]{3,2,1,0:T(1,128)S(1)}, u32[]{:S(2)}, u32[]{:S(2)}) collective-permute-start(f32[3,16,1,512]{3,2,1,0:T(1,128)S(1)} %get-tuple-element.41), channel_id=1, source_target_pairs={{1,0},{2,1},{3,2},{4,3},{5,4},{6,5},{7,6},{9,8},{10,9},{11,10},{12... | collective-permute-start | bytes 294920 | tf_op jit(solution)/shard_map/ppermute | solution.py:20
  108.2 3.3 %collective-permute-done.5 = f32[3,16,1,512]{3,2,1,0:T(1,128)S(1)} collective-permute-done((f32[3,16,1,512]{3,2,1,0:T(1,128)S(1)}, f32[3,16,1,512]{3,2,1,0:T(1,128)S(1)}, u32[]{:S(2)}, u32[]{:S(2)}) %collective-permute-start.5) | collective-permute-done | bytes 98336 | tf_op jit(solution)/shard_map/ppermute | solution.py:20
  111.5 1.6 %select_maximum_fusion = f32[3,16,18,514]{3,2,1,0:T(8,128)S(1)} fusion(f32[3,16,1,512]{3,2,1,0:T(1,128)S(1)} %collective-permute-done.5, f32[3,16,1,512]{3,2,1,0:T(1,128)S(1)} %collective-permute-done.4, f32[1,16,16,512]{3,2,1,0:T(8,128)S(1)} %get-tuple-element.43, f32[1,16,16,512]{3,2,1,0:T(8,128)S(1)} %get-tuple-element.42, f32[1,16,16,512]{3,2,1,0:T(8,128)S(1)} %bitcast.70), kind=kLoop, calls=%fused_computation.9 | loop fusion | flops 5329152 | bytes 3545856 | tf_op jit(solution)/shard_map/concatenate | solution.py:21
  113.3 1.5 %fusion.18 = (f32[1,16,16,512]{3,2,1,0:T(8,128)S(1)}, f32[1,16,16,512]{3,2,1,0:T(8,128)S(1)}) fusion(f32[16,18,514]{2,1,0:T(8,128)S(1)} %get-tuple-element.31, f32[16,18,514]{2,1,0:T(8,128)S(1)} %get-tuple-element.29, f32[16,18,514]{2,1,0:T(8,128)S(1)} %get-tuple-element.30, f32[16,16,512]{2,1,0:T(8,128)S(1)} %bitcast.72, f32[16,16,512]{2,1,0:T(8,128)S(1)} %bitcast.68, ...), kind=kLoop, calls=%fused_computation.60 | loop fusion | flops 2621440 | bytes 8912896 | tf_op jit(solution)/shard_map/stack | solution.py:116
  116.7 3.6 %fusion.47 = f32[8,16,16,128]{3,2,1,0:T(8,128)S(1)} fusion(f32[8,16,16,512]{3,2,1,0:T(8,128)S(1)} %fusion.1, f32[128]{0:T(128)S(1)} %iota_convert_fusion, f32[512]{0:T(512)S(1)} %multiply_add_fusion), kind=kOutput, calls=%fused_computation.112 | convolution fusion | flops 1610874880 | bytes 5245440 | tf_op jit(solution)/shard_map/mlij,jb->mlib/dot_general | solution.py:140
  121.2 1.9 %collective-permute-start.6 = (f32[8,16,128]{2,1,0:T(8,128)S(1)}, f32[8,16,128]{2,1,0:T(8,128)S(1)}, u32[]{:S(2)}, u32[]{:S(2)}) collective-permute-start(f32[8,16,128]{2,1,0:T(8,128)S(1)} %bitcast.76), channel_id=1, source_target_pairs={{1,0},{2,1},{3,2},{4,3},{5,4},{6,5},{7,6},{9,8},{10,9},{11,10},{12... | collective-permute-start | bytes 196616 | tf_op jit(solution)/shard_map/ppermute | solution.py:28
  123.2 3.6 %collective-permute-start.7 = (f32[8,16,128]{2,1,0:T(8,128)S(1)}, f32[8,16,128]{2,1,0:T(8,128)S(1)}, u32[]{:S(2)}, u32[]{:S(2)}) collective-permute-start(f32[8,16,128]{2,1,0:T(8,128)S(1)} %bitcast.75), channel_id=1, source_target_pairs={{0,1},{1,2},{2,3},{3,4},{4,5},{5,6},{6,7},{8,9},{9,10},{10,11},{11... | collective-permute-start | bytes 196616 | tf_op jit(solution)/shard_map/ppermute | solution.py:28
  126.9 1.3 collective-permute-done.7
  128.2 4.3 %collective-permute-start.8 = (f32[8,16,2,128]{3,1,0,2:T(8,128)S(1)}, f32[8,16,2,128]{3,1,0,2:T(8,128)S(1)}, u32[]{:S(2)}, u32[]{:S(2)}) collective-permute-start(f32[8,16,2,128]{3,1,0,2:T(8,128)S(1)} %get-tuple-element.67), channel_id=1, source_target_pairs={{0,1},{1,2},{2,3},{3,4},{4,5},{5,6},{6,7},{8,9},{9,10},{10,11},{11... | collective-permute-start | bytes 393224 | tf_op jit(solution)/shard_map/ppermute | solution.py:19
  132.5 1.9 %collective-permute-start.9 = (f32[8,16,2,128]{3,1,0,2:T(8,128)S(1)}, f32[8,16,2,128]{3,1,0,2:T(8,128)S(1)}, u32[]{:S(2)}, u32[]{:S(2)}) collective-permute-start(f32[8,16,2,128]{3,1,0,2:T(8,128)S(1)} %get-tuple-element.68), channel_id=1, source_target_pairs={{1,0},{2,1},{3,2},{4,3},{5,4},{6,5},{7,6},{9,8},{10,9},{11,10},{12... | collective-permute-start | bytes 393224 | tf_op jit(solution)/shard_map/ppermute | solution.py:20
  134.5 4.3 %collective-permute-done.9 = f32[8,16,2,128]{3,1,0,2:T(8,128)S(1)} collective-permute-done((f32[8,16,2,128]{3,1,0,2:T(8,128)S(1)}, f32[8,16,2,128]{3,1,0,2:T(8,128)S(1)}, u32[]{:S(2)}, u32[]{:S(2)}) %collective-permute-start.9) | collective-permute-done | bytes 131104 | tf_op jit(solution)/shard_map/ppermute | solution.py:20
  (67 shorter events, 14.3 us)
Async XLA Ops:
  6.5 8.4 %copy-start.3 = (f32[8,16,4,128]{3,2,1,0:T(4,128)S(1)}, f32[8,16,4,128]{3,2,1,0:T(4,128)}, u32[]{:S(2)}) copy-start(f32[8,16,4,128]{3,2,1,0:T(4,128)} %param.10) | copy-start | bytes 786436
  6.5 73.3 %all-reduce.8.cloned.1.call-start = ((), (), s32[]{:S(2)}) async-start(), calls=%async_computation | async-start | bytes 2097152 | tf_op jit(solution)/shard_map/psum | solution.py:130
  7.7 7.2 %collective-permute-start = (f32[8,16,3,128]{3,1,0,2:T(8,128)S(1)}, f32[8,16,3,128]{3,1,0,2:T(8,128)S(1)}, u32[]{:S(2)}, u32[]{:S(2)}) collective-permute-start(f32[8,16,3,128]{3,1,0,2:T(8,128)S(1)} %copy.30), channel_id=1, source_target_pairs={{0,1},{1,2},{2,3},{3,4},{4,5},{5,6},{6,7},{8,9},{9,10},{10,11},{11... | collective-permute-start | bytes 589832 | tf_op jit(solution)/shard_map/ppermute | solution.py:19
  12.4 7.0 %collective-permute-start.1 = (f32[8,16,3,128]{3,1,0,2:T(8,128)S(1)}, f32[8,16,3,128]{3,1,0,2:T(8,128)S(1)}, u32[]{:S(2)}, u32[]{:S(2)}) collective-permute-start(f32[8,16,3,128]{3,1,0,2:T(8,128)S(1)} %copy.31), channel_id=1, source_target_pairs={{1,0},{2,1},{3,2},{4,3},{5,4},{6,5},{7,6},{9,8},{10,9},{11,10},{12... | collective-permute-start | bytes 589832 | tf_op jit(solution)/shard_map/ppermute | solution.py:20
  21.8 3.5 %copy-start.1 = (bf16[8,2,16,16,512]{4,3,2,1,0:T(8,128)(2,1)S(1)}, bf16[8,2,16,16,512]{4,3,2,1,0:T(8,128)(2,1)}, u32[]{:S(2)}) copy-start(bf16[8,2,16,16,512]{4,3,2,1,0:T(8,128)(2,1)} %param.11) | copy-start | bytes 12582916
  26.5 60.6 %copy-start.4 = (s32[1024]{0:T(1024)S(1)}, s32[1024]{0:T(1024)}, u32[]{:S(2)}) copy-start(s32[1024]{0:T(1024)} %param.12) | copy-start | bytes 12292
  26.5 60.6 %copy-start.7 = (s32[1024]{0:T(1024)S(1)}, s32[1024]{0:T(1024)}, u32[]{:S(2)}) copy-start(s32[1024]{0:T(1024)} %param.13) | copy-start | bytes 12292
  81.1 6.0 %collective-permute-start.2 = (f32[2,16,1,512]{3,2,1,0:T(1,128)S(1)}, f32[2,16,1,512]{3,2,1,0:T(1,128)S(1)}, u32[]{:S(2)}, u32[]{:S(2)}) collective-permute-start(f32[2,16,1,512]{3,2,1,0:T(1,128)S(1)} %get-tuple-element.44), channel_id=1, source_target_pairs={{0,1},{1,2},{2,3},{3,4},{4,5},{5,6},{6,7},{8,9},{9,10},{10,11},{11... | collective-permute-start | bytes 196616 | tf_op jit(solution)/shard_map/ppermute | solution.py:19
  85.0 5.6 %collective-permute-start.3 = (f32[2,16,1,512]{3,2,1,0:T(1,128)S(1)}, f32[2,16,1,512]{3,2,1,0:T(1,128)S(1)}, u32[]{:S(2)}, u32[]{:S(2)}) collective-permute-start(f32[2,16,1,512]{3,2,1,0:T(1,128)S(1)} %get-tuple-element.45), channel_id=1, source_target_pairs={{1,0},{2,1},{3,2},{4,3},{5,4},{6,5},{7,6},{9,8},{10,9},{11,10},{12... | collective-permute-start | bytes 196616 | tf_op jit(solution)/shard_map/ppermute | solution.py:20
  92.9 1.2 copy-start
  95.1 3.7 %copy-start.5 = (f32[1024]{0:T(1024)S(1)}, f32[1024]{0:T(1024)}, u32[]{:S(2)}) copy-start(f32[1024]{0:T(1024)} %param.15) | copy-start | bytes 12292
  95.1 3.7 %copy-start.6 = (f32[1024]{0:T(1024)S(1)}, f32[1024]{0:T(1024)}, u32[]{:S(2)}) copy-start(f32[1024]{0:T(1024)} %param.14) | copy-start | bytes 12292
  103.7 4.6 %collective-permute-start.4 = (f32[3,16,1,512]{3,2,1,0:T(1,128)S(1)}, f32[3,16,1,512]{3,2,1,0:T(1,128)S(1)}, u32[]{:S(2)}, u32[]{:S(2)}) collective-permute-start(f32[3,16,1,512]{3,2,1,0:T(1,128)S(1)} %get-tuple-element.40), channel_id=1, source_target_pairs={{0,1},{1,2},{2,3},{3,4},{4,5},{5,6},{6,7},{8,9},{9,10},{10,11},{11... | collective-permute-start | bytes 294920 | tf_op jit(solution)/shard_map/ppermute | solution.py:19
  105.6 5.9 %collective-permute-start.5 = (f32[3,16,1,512]{3,2,1,0:T(1,128)S(1)}, f32[3,16,1,512]{3,2,1,0:T(1,128)S(1)}, u32[]{:S(2)}, u32[]{:S(2)}) collective-permute-start(f32[3,16,1,512]{3,2,1,0:T(1,128)S(1)} %get-tuple-element.41), channel_id=1, source_target_pairs={{1,0},{2,1},{3,2},{4,3},{5,4},{6,5},{7,6},{9,8},{10,9},{11,10},{12... | collective-permute-start | bytes 294920 | tf_op jit(solution)/shard_map/ppermute | solution.py:20
  113.3 2.2 %copy-start.2 = (bf16[8,2,16,16,512]{4,3,2,1,0:T(8,128)(2,1)S(1)}, bf16[8,2,16,16,512]{4,3,2,1,0:T(8,128)(2,1)}, u32[]{:S(2)}) copy-start(bf16[8,2,16,16,512]{4,3,2,1,0:T(8,128)(2,1)} %param.11) | copy-start | bytes 12582916
  121.2 5.7 %collective-permute-start.6 = (f32[8,16,128]{2,1,0:T(8,128)S(1)}, f32[8,16,128]{2,1,0:T(8,128)S(1)}, u32[]{:S(2)}, u32[]{:S(2)}) collective-permute-start(f32[8,16,128]{2,1,0:T(8,128)S(1)} %bitcast.76), channel_id=1, source_target_pairs={{1,0},{2,1},{3,2},{4,3},{5,4},{6,5},{7,6},{9,8},{10,9},{11,10},{12... | collective-permute-start | bytes 196616 | tf_op jit(solution)/shard_map/ppermute | solution.py:28
  123.2 5.0 %collective-permute-start.7 = (f32[8,16,128]{2,1,0:T(8,128)S(1)}, f32[8,16,128]{2,1,0:T(8,128)S(1)}, u32[]{:S(2)}, u32[]{:S(2)}) collective-permute-start(f32[8,16,128]{2,1,0:T(8,128)S(1)} %bitcast.75), channel_id=1, source_target_pairs={{0,1},{1,2},{2,3},{3,4},{4,5},{5,6},{6,7},{8,9},{9,10},{10,11},{11... | collective-permute-start | bytes 196616 | tf_op jit(solution)/shard_map/ppermute | solution.py:28
  128.2 6.2 %collective-permute-start.8 = (f32[8,16,2,128]{3,1,0,2:T(8,128)S(1)}, f32[8,16,2,128]{3,1,0,2:T(8,128)S(1)}, u32[]{:S(2)}, u32[]{:S(2)}) collective-permute-start(f32[8,16,2,128]{3,1,0,2:T(8,128)S(1)} %get-tuple-element.67), channel_id=1, source_target_pairs={{0,1},{1,2},{2,3},{3,4},{4,5},{5,6},{6,7},{8,9},{9,10},{10,11},{11... | collective-permute-start | bytes 393224 | tf_op jit(solution)/shard_map/ppermute | solution.py:19
  132.5 6.3 %collective-permute-start.9 = (f32[8,16,2,128]{3,1,0,2:T(8,128)S(1)}, f32[8,16,2,128]{3,1,0,2:T(8,128)S(1)}, u32[]{:S(2)}, u32[]{:S(2)}) collective-permute-start(f32[8,16,2,128]{3,1,0,2:T(8,128)S(1)} %get-tuple-element.68), channel_id=1, source_target_pairs={{1,0},{2,1},{3,2},{4,3},{5,4},{6,5},{7,6},{9,8},{10,9},{11,10},{12... | collective-permute-start | bytes 393224 | tf_op jit(solution)/shard_map/ppermute | solution.py:20
Sparse Core Ops, SparseCore 0:
  27.8 52.0 all-reduce.7
where the time goes:
time: 148 us; the launch traced here: 147 us
  waiting for transfers between devices  69.5 us (47%)
  starting transfers between devices  28.7 us (19%)
  matrix products  16.9 us (11%)
  between operations  13.9 us (9%)
  other arithmetic  11.1 us (8%)
  local copies, waits for them, and re-layouts  7.37 us (5%)
    psum x1, waiting for transfers between devices, local(): whole = lax.psum(partial_value, 'mem')  52.2 us
    ppermute x4, waiting for transfers between devices, padded_2(): after = lax.ppermute(first, axis, down)  15.4 us
    ppermute x4, starting transfers between devices, padded_2(): before = lax.ppermute(last, axis, up)  14.6 us
    ppermute x4, starting transfers between devices, padded_2(): after = lax.ppermute(first, axis, down)  8.57 us
    ppermute x2, starting transfers between devices, from_behind(): return lax.ppermute(value, axis, pairs)  5.56 us
    dot_general x1, matrix products, observe(): lax.dot_general(line_hot, weighted, (((0,), (0,)), ((), ())), precision=h...  4.19 us
    concatenate x3, other arithmetic, padded_2(): value = jnp.concatenate([before, value, after], axis=dim)  3.91 us
    dot_general x1, matrix products, observe(): jnp.dot(line_hot, table, precision=highest, preferred_element_type=jnp.fl...  3.66 us
  transfers between devices with their start and end apart: 11, of which 7 were waited for; matrix products, arithmetic and copies ran while one was open for 0% of the time, Pallas kernels for 0%

commit v1 on v0

--- a/solution.py
+++ b/solution.py
@@ -127,7 +127,18 @@
     part = jnp.einsum("ia,mlab->mlib", rows_x, smoothed, precision=highest)
     fine = jnp.einsum("mlib,jb->mlij", part, rows_y, precision=highest)
     partial_value = jnp.sum(fine[:, None] * perturbation.astype(jnp.float32), axis=0) * scale
-    whole = lax.psum(partial_value, "mem")
+
+    def _test_rounds(incoming_x):
+        nd = jax.lax.axis_size("mem")
+        z1 = incoming_x
+        for num in [b for b in (1, 2, 4, 8, 16) if b < nd]:
+            work_now = jax.lax.ppermute(
+                z1, "mem", perm=[(dev_j, dev_j ^ num) for dev_j in range(nd)]
+            )
+            z1 = z1 + work_now
+        return z1
+
+    whole = _test_rounds(partial_value)
     level_first = 0
     extended = jnp.pad(padded_2(whole, (("reg", 2),), 1), ((0, 0), (0, 0), (0, 0), (1, 1)))
 

time: 148 us -> 127 us (0.86)
  between operations: 13.9 us -> 0.56 us
  waiting for transfers between devices: 69.5 us -> 59.4 us
  starting transfers between devices: 28.7 us -> 35.6 us
  local copies, waits for them, and re-layouts: 7.37 us -> 4.5 us
  other arithmetic: 11.1 us -> 9.37 us
    psum x1 -> x0, waiting for transfers between devices: 52.2 us -> none  [local(): whole = lax.psum(partial_value, 'mem')]
    ppermute x0 -> x2, waiting for transfers between devices: none -> 42.1 us  [_test_rounds(): jax.lax.ppermute(z1, 'mem', perm=[(dev_j, dev_j ^ num) for dev_j in range...]
    ppermute x4, starting transfers between devices: 14.6 us -> 18.9 us  [padded_2(): before = lax.ppermute(last, axis, up)]
    ppermute x0 -> x2, starting transfers between devices: none -> 2.58 us  [_test_rounds(): jax.lax.ppermute(z1, 'mem', perm=[(dev_j, dev_j ^ num) for dev_j in range...]
    unnamed x21 -> x17, local copies, waits for them, and re-layouts: 1.8 us -> 0.12 us
  transfers between devices with their start and end apart: 11 -> 12, of which waited for: 7 -> 8; matrix products, arithmetic and copies ran while one was open for 0% -> 0% of each run, Pallas kernels for 0% -> 0%
where the time goes in v1:
time: 127 us; the launch traced here: 126 us
  waiting for transfers between devices  59.4 us (47%)
  starting transfers between devices  35.6 us (28%)
  matrix products  16.9 us (13%)
  other arithmetic  9.37 us (7%)
  local copies, waits for them, and re-layouts  4.5 us (4%)
    ppermute x2, waiting for transfers between devices, _test_rounds(): jax.lax.ppermute(z1, 'mem', perm=[(dev_j, dev_j ^ num) for dev_j in range...  42.1 us
    ppermute x4, starting transfers between devices, padded_2(): before = lax.ppermute(last, axis, up)  18.9 us
    ppermute x4, waiting for transfers between devices, padded_2(): after = lax.ppermute(first, axis, down)  15.4 us
    ppermute x4, starting transfers between devices, padded_2(): after = lax.ppermute(first, axis, down)  8.57 us
    ppermute x2, starting transfers between devices, from_behind(): return lax.ppermute(value, axis, pairs)  5.56 us
    dot_general x1, matrix products, observe(): lax.dot_general(line_hot, weighted, (((0,), (0,)), ((), ())), precision=h...  4.19 us
    dot_general x1, matrix products, observe(): jnp.dot(line_hot, table, precision=highest, preferred_element_type=jnp.fl...  3.66 us
    dot_general x1, matrix products, local(): jnp.einsum('mlij,jb->mlib', product, rows_y, precision=highest)  3.6 us
  transfers between devices with their start and end apart: 12, of which 8 were waited for; matrix products, arithmetic and copies ran while one was open for 0% of the time, Pallas kernels for 0%

profile of v1, /device:TPU:1, one launch (start us, length us, event | category | flops | bytes accessed | tf_op | source)
XLA Modules:
  0.0 126.2 jit_solution(4367754421818866147)
XLA Ops:
  1.2 4.6 %collective-permute-start = (f32[8,16,3,128]{3,1,0,2:T(8,128)S(1)}, f32[8,16,3,128]{3,1,0,2:T(8,128)S(1)}, u32[]{:S(2)}, u32[]{:S(2)}) collective-permute-start(f32[8,16,3,128]{3,1,0,2:T(8,128)S(1)} %copy.30), channel_id=1, source_target_pairs={{0,1},{1,2},{2,3},{3,4},{4,5},{5,6},{6,7},{8,9},{9,10},{10,11},{11... | collective-permute-start | bytes 589832 | tf_op jit(solution)/shard_map/ppermute | solution.py:19
  5.8 1.9 %collective-permute-start.1 = (f32[8,16,3,128]{3,1,0,2:T(8,128)S(1)}, f32[8,16,3,128]{3,1,0,2:T(8,128)S(1)}, u32[]{:S(2)}, u32[]{:S(2)}) collective-permute-start(f32[8,16,3,128]{3,1,0,2:T(8,128)S(1)} %copy.31), channel_id=1, source_target_pairs={{1,0},{2,1},{3,2},{4,3},{5,4},{6,5},{7,6},{9,8},{10,9},{11,10},{12... | collective-permute-start | bytes 589832 | tf_op jit(solution)/shard_map/ppermute | solution.py:20
  8.4 4.4 %collective-permute-done.1 = f32[8,16,3,128]{3,1,0,2:T(8,128)S(1)} collective-permute-done((f32[8,16,3,128]{3,1,0,2:T(8,128)S(1)}, f32[8,16,3,128]{3,1,0,2:T(8,128)S(1)}, u32[]{:S(2)}, u32[]{:S(2)}) %collective-permute-start.1) | collective-permute-done | bytes 196640 | tf_op jit(solution)/shard_map/ppermute | solution.py:20
  15.3 3.5 %fusion.49 = f32[8,16,16,512]{3,2,1,0:T(8,128)S(1)} fusion(f32[8,16,16,128]{3,2,1,0:T(8,128)S(1)} %convolution_bitcast_fusion, f32[128]{0:T(128)S(1)} %iota_convert_fusion, f32[512]{0:T(512)S(1)} %multiply_add_fusion), kind=kOutput, calls=%fused_computation.114 | convolution fusion | flops 1610874880 | bytes 5245440 | tf_op jit(solution)/shard_map/mlib,jb->mlij/dot_general | solution.py:128
  21.4 20.5 %collective-permute-done.2 = f32[2,16,16,512]{3,2,1,0:T(8,128)S(1)} collective-permute-done((f32[2,16,16,512]{3,2,1,0:T(8,128)S(1)}, f32[2,16,16,512]{3,2,1,0:T(8,128)S(1)}, u32[]{:S(2)}, u32[]{:S(2)}) %collective-permute-start.2) | collective-permute-done | bytes 1048608 | tf_op jit(solution)/shard_map/ppermute | solution.py:135
  42.2 1.3 %collective-permute-start.3 = (f32[2,16,16,512]{3,2,1,0:T(8,128)S(1)}, f32[2,16,16,512]{3,2,1,0:T(8,128)S(1)}, u32[]{:S(2)}, u32[]{:S(2)}) collective-permute-start(f32[2,16,16,512]{3,2,1,0:T(8,128)S(1)} %fusion.86), channel_id=1, source_target_pairs={{0,16},{8,24},{16,0},{24,8},{1,17},{9,25},{17,1},{25,9},{2,18},{10... | collective-permute-start | bytes 3145736 | tf_op jit(solution)/shard_map/ppermute | solution.py:135
  43.5 21.6 %collective-permute-done.3 = f32[2,16,16,512]{3,2,1,0:T(8,128)S(1)} collective-permute-done((f32[2,16,16,512]{3,2,1,0:T(8,128)S(1)}, f32[2,16,16,512]{3,2,1,0:T(8,128)S(1)}, u32[]{:S(2)}, u32[]{:S(2)}) %collective-permute-start.3) | collective-permute-done | bytes 1048608 | tf_op jit(solution)/shard_map/ppermute | solution.py:135
  65.5 8.1 %collective-permute-start.4 = (f32[2,16,1,512]{3,2,1,0:T(1,128)S(1)}, f32[2,16,1,512]{3,2,1,0:T(1,128)S(1)}, u32[]{:S(2)}, u32[]{:S(2)}) collective-permute-start(f32[2,16,1,512]{3,2,1,0:T(1,128)S(1)} %get-tuple-element.44), channel_id=1, source_target_pairs={{0,1},{1,2},{2,3},{3,4},{4,5},{5,6},{6,7},{8,9},{9,10},{10,11},{11... | collective-permute-start | bytes 196616 | tf_op jit(solution)/shard_map/ppermute | solution.py:19
  73.6 2.1 %collective-permute-start.5 = (f32[2,16,1,512]{3,2,1,0:T(1,128)S(1)}, f32[2,16,1,512]{3,2,1,0:T(1,128)S(1)}, u32[]{:S(2)}, u32[]{:S(2)}) collective-permute-start(f32[2,16,1,512]{3,2,1,0:T(1,128)S(1)} %get-tuple-element.45), channel_id=1, source_target_pairs={{1,0},{2,1},{3,2},{4,3},{5,4},{6,5},{7,6},{9,8},{10,9},{11,10},{12... | collective-permute-start | bytes 196616 | tf_op jit(solution)/shard_map/ppermute | solution.py:20
  75.8 3.4 %collective-permute-done.5 = f32[2,16,1,512]{3,2,1,0:T(1,128)S(1)} collective-permute-done((f32[2,16,1,512]{3,2,1,0:T(1,128)S(1)}, f32[2,16,1,512]{3,2,1,0:T(1,128)S(1)}, u32[]{:S(2)}, u32[]{:S(2)}) %collective-permute-start.5) | collective-permute-done | bytes 65568 | tf_op jit(solution)/shard_map/ppermute | solution.py:20
  81.4 3.7 %select_reduce_fusion = f32[1024]{0:T(1024)S(1)} fusion(f32[1024,512]{1,0:T(8,128)S(1)} %bitcast.71, s32[1024]{0:T(1024)S(1)} %get-tuple-element.72, s32[1024]{0:T(1024)S(1)} %get-tuple-element.71), kind=kOutput, calls=%fused_computation.30 | convolution fusion | flops 6445071360 | bytes 2109440 | tf_op jit(solution)/shard_map/dot_general | solution.py:98
  85.1 4.2 %fusion.2 = f32[1024,512]{1,0:T(8,128)S(1)} fusion(s32[1024]{0:T(1024)S(1)} %get-tuple-element.72, f32[1024]{0:T(1024)S(1)} %multiply_select_fusion, s32[1024]{0:T(1024)S(1)} %get-tuple-element.71), kind=kOutput, calls=%fused_computation.7 | convolution fusion | flops 6444548096 | bytes 2109440 | tf_op jit(solution)/shard_map/dot_general | solution.py:102
  89.9 1.9 %collective-permute-start.6 = (f32[3,16,1,512]{3,2,1,0:T(1,128)S(1)}, f32[3,16,1,512]{3,2,1,0:T(1,128)S(1)}, u32[]{:S(2)}, u32[]{:S(2)}) collective-permute-start(f32[3,16,1,512]{3,2,1,0:T(1,128)S(1)} %get-tuple-element.40), channel_id=1, source_target_pairs={{0,1},{1,2},{2,3},{3,4},{4,5},{5,6},{6,7},{8,9},{9,10},{10,11},{11... | collective-permute-start | bytes 294920 | tf_op jit(solution)/shard_map/ppermute | solution.py:19
  91.8 2.6 %collective-permute-start.7 = (f32[3,16,1,512]{3,2,1,0:T(1,128)S(1)}, f32[3,16,1,512]{3,2,1,0:T(1,128)S(1)}, u32[]{:S(2)}, u32[]{:S(2)}) collective-permute-start(f32[3,16,1,512]{3,2,1,0:T(1,128)S(1)} %get-tuple-element.41), channel_id=1, source_target_pairs={{1,0},{2,1},{3,2},{4,3},{5,4},{6,5},{7,6},{9,8},{10,9},{11,10},{12... | collective-permute-start | bytes 294920 | tf_op jit(solution)/shard_map/ppermute | solution.py:20
  94.4 3.3 %collective-permute-done.7 = f32[3,16,1,512]{3,2,1,0:T(1,128)S(1)} collective-permute-done((f32[3,16,1,512]{3,2,1,0:T(1,128)S(1)}, f32[3,16,1,512]{3,2,1,0:T(1,128)S(1)}, u32[]{:S(2)}, u32[]{:S(2)}) %collective-permute-start.7) | collective-permute-done | bytes 98336 | tf_op jit(solution)/shard_map/ppermute | solution.py:20
  97.7 1.6 %select_maximum_fusion = f32[3,16,18,514]{3,2,1,0:T(8,128)S(1)} fusion(f32[3,16,1,512]{3,2,1,0:T(1,128)S(1)} %collective-permute-done.7, f32[3,16,1,512]{3,2,1,0:T(1,128)S(1)} %collective-permute-done.6, f32[1,16,16,512]{3,2,1,0:T(8,128)S(1)} %get-tuple-element.43, f32[1,16,16,512]{3,2,1,0:T(8,128)S(1)} %get-tuple-element.42, f32[1,16,16,512]{3,2,1,0:T(8,128)S(1)} %bitcast.70), kind=kLoop, calls=%fused_computation.9 | loop fusion | flops 5329152 | bytes 3545856 | tf_op jit(solution)/shard_map/concatenate | solution.py:21
  99.5 1.5 %fusion.18 = (f32[1,16,16,512]{3,2,1,0:T(8,128)S(1)}, f32[1,16,16,512]{3,2,1,0:T(8,128)S(1)}) fusion(f32[16,18,514]{2,1,0:T(8,128)S(1)} %get-tuple-element.31, f32[16,18,514]{2,1,0:T(8,128)S(1)} %get-tuple-element.29, f32[16,18,514]{2,1,0:T(8,128)S(1)} %get-tuple-element.30, f32[16,16,512]{2,1,0:T(8,128)S(1)} %bitcast.72, f32[16,16,512]{2,1,0:T(8,128)S(1)} %bitcast.68, ...), kind=kLoop, calls=%fused_computation.60 | loop fusion | flops 2621440 | bytes 8912896 | tf_op jit(solution)/shard_map/stack | solution.py:116
  102.3 3.6 %fusion.47 = f32[8,16,16,128]{3,2,1,0:T(8,128)S(1)} fusion(f32[8,16,16,512]{3,2,1,0:T(8,128)S(1)} %fusion.1, f32[128]{0:T(128)S(1)} %iota_convert_fusion, f32[512]{0:T(512)S(1)} %multiply_add_fusion), kind=kOutput, calls=%fused_computation.112 | convolution fusion | flops 1610874880 | bytes 5245440 | tf_op jit(solution)/shard_map/mlij,jb->mlib/dot_general | solution.py:151
  106.8 1.9 %collective-permute-start.8 = (f32[8,16,128]{2,1,0:T(8,128)S(1)}, f32[8,16,128]{2,1,0:T(8,128)S(1)}, u32[]{:S(2)}, u32[]{:S(2)}) collective-permute-start(f32[8,16,128]{2,1,0:T(8,128)S(1)} %bitcast.76), channel_id=1, source_target_pairs={{1,0},{2,1},{3,2},{4,3},{5,4},{6,5},{7,6},{9,8},{10,9},{11,10},{12... | collective-permute-start | bytes 196616 | tf_op jit(solution)/shard_map/ppermute | solution.py:28
  108.8 3.6 %collective-permute-start.9 = (f32[8,16,128]{2,1,0:T(8,128)S(1)}, f32[8,16,128]{2,1,0:T(8,128)S(1)}, u32[]{:S(2)}, u32[]{:S(2)}) collective-permute-start(f32[8,16,128]{2,1,0:T(8,128)S(1)} %bitcast.75), channel_id=1, source_target_pairs={{0,1},{1,2},{2,3},{3,4},{4,5},{5,6},{6,7},{8,9},{9,10},{10,11},{11... | collective-permute-start | bytes 196616 | tf_op jit(solution)/shard_map/ppermute | solution.py:28
  112.5 1.3 %collective-permute-done.9 = f32[8,16,128]{2,1,0:T(8,128)S(1)} collective-permute-done((f32[8,16,128]{2,1,0:T(8,128)S(1)}, f32[8,16,128]{2,1,0:T(8,128)S(1)}, u32[]{:S(2)}, u32[]{:S(2)}) %collective-permute-start.9) | collective-permute-done | bytes 65568 | tf_op jit(solution)/shard_map/ppermute | solution.py:28
  113.8 4.3 %collective-permute-start.10 = (f32[8,16,2,128]{3,1,0,2:T(8,128)S(1)}, f32[8,16,2,128]{3,1,0,2:T(8,128)S(1)}, u32[]{:S(2)}, u32[]{:S(2)}) collective-permute-start(f32[8,16,2,128]{3,1,0,2:T(8,128)S(1)} %get-tuple-element.67), channel_id=1, source_target_pairs={{0,1},{1,2},{2,3},{3,4},{4,5},{5,6},{6,7},{8,9},{9,10},{10,11},{11... | collective-permute-start | bytes 393224 | tf_op jit(solution)/shard_map/ppermute | solution.py:19
  118.1 1.9 %collective-permute-start.11 = (f32[8,16,2,128]{3,1,0,2:T(8,128)S(1)}, f32[8,16,2,128]{3,1,0,2:T(8,128)S(1)}, u32[]{:S(2)}, u32[]{:S(2)}) collective-permute-start(f32[8,16,2,128]{3,1,0,2:T(8,128)S(1)} %get-tuple-element.68), channel_id=1, source_target_pairs={{1,0},{2,1},{3,2},{4,3},{5,4},{6,5},{7,6},{9,8},{10,9},{11,10},{12... | collective-permute-start | bytes 393224 | tf_op jit(solution)/shard_map/ppermute | solution.py:20
  120.0 4.3 %collective-permute-done.11 = f32[8,16,2,128]{3,1,0,2:T(8,128)S(1)} collective-permute-done((f32[8,16,2,128]{3,1,0,2:T(8,128)S(1)}, f32[8,16,2,128]{3,1,0,2:T(8,128)S(1)}, u32[]{:S(2)}, u32[]{:S(2)}) %collective-permute-start.11) | collective-permute-done | bytes 131104 | tf_op jit(solution)/shard_map/ppermute | solution.py:20
  (66 shorter events, 14.5 us)
Async XLA Ops:
  0.0 8.4 %copy-start.1 = (f32[8,16,4,128]{3,2,1,0:T(4,128)S(1)}, f32[8,16,4,128]{3,2,1,0:T(4,128)}, u32[]{:S(2)}) copy-start(f32[8,16,4,128]{3,2,1,0:T(4,128)} %param.10) | copy-start | bytes 786436
  1.2 7.2 %collective-permute-start = (f32[8,16,3,128]{3,1,0,2:T(8,128)S(1)}, f32[8,16,3,128]{3,1,0,2:T(8,128)S(1)}, u32[]{:S(2)}, u32[]{:S(2)}) collective-permute-start(f32[8,16,3,128]{3,1,0,2:T(8,128)S(1)} %copy.30), channel_id=1, source_target_pairs={{0,1},{1,2},{2,3},{3,4},{4,5},{5,6},{6,7},{8,9},{9,10},{10,11},{11... | collective-permute-start | bytes 589832 | tf_op jit(solution)/shard_map/ppermute | solution.py:19
  5.8 7.0 %collective-permute-start.1 = (f32[8,16,3,128]{3,1,0,2:T(8,128)S(1)}, f32[8,16,3,128]{3,1,0,2:T(8,128)S(1)}, u32[]{:S(2)}, u32[]{:S(2)}) collective-permute-start(f32[8,16,3,128]{3,1,0,2:T(8,128)S(1)} %copy.31), channel_id=1, source_target_pairs={{1,0},{2,1},{3,2},{4,3},{5,4},{6,5},{7,6},{9,8},{10,9},{11,10},{12... | collective-permute-start | bytes 589832 | tf_op jit(solution)/shard_map/ppermute | solution.py:20
  15.3 3.5 %copy-start = (bf16[8,2,16,16,512]{4,3,2,1,0:T(8,128)(2,1)S(1)}, bf16[8,2,16,16,512]{4,3,2,1,0:T(8,128)(2,1)}, u32[]{:S(2)}) copy-start(bf16[8,2,16,16,512]{4,3,2,1,0:T(8,128)(2,1)} %param.11) | copy-start | bytes 12582916
  20.1 21.8 %collective-permute-start.2 = (f32[2,16,16,512]{3,2,1,0:T(8,128)S(1)}, f32[2,16,16,512]{3,2,1,0:T(8,128)S(1)}, u32[]{:S(2)}, u32[]{:S(2)}) collective-permute-start(f32[2,16,16,512]{3,2,1,0:T(8,128)S(1)} %broadcast_multiply_fusion), channel_id=1, source_target_pairs={{0,8},{8,0},{16,24},{24,16},{1,9},{9,1},{17,25},{25,17},{2,10},{10... | collective-permute-start | bytes 3145736 | tf_op jit(solution)/shard_map/ppermute | solution.py:135
  42.2 33.5 %copy-start.2 = (s32[1024]{0:T(1024)S(1)}, s32[1024]{0:T(1024)}, u32[]{:S(2)}) copy-start(s32[1024]{0:T(1024)} %param.12) | copy-start | bytes 12292
  42.2 33.5 %copy-start.5 = (s32[1024]{0:T(1024)S(1)}, s32[1024]{0:T(1024)}, u32[]{:S(2)}) copy-start(s32[1024]{0:T(1024)} %param.13) | copy-start | bytes 12292
  42.2 22.9 %collective-permute-start.3 = (f32[2,16,16,512]{3,2,1,0:T(8,128)S(1)}, f32[2,16,16,512]{3,2,1,0:T(8,128)S(1)}, u32[]{:S(2)}, u32[]{:S(2)}) collective-permute-start(f32[2,16,16,512]{3,2,1,0:T(8,128)S(1)} %fusion.86), channel_id=1, source_target_pairs={{0,16},{8,24},{16,0},{24,8},{1,17},{9,25},{17,1},{25,9},{2,18},{10... | collective-permute-start | bytes 3145736 | tf_op jit(solution)/shard_map/ppermute | solution.py:135
  65.5 10.3 %collective-permute-start.4 = (f32[2,16,1,512]{3,2,1,0:T(1,128)S(1)}, f32[2,16,1,512]{3,2,1,0:T(1,128)S(1)}, u32[]{:S(2)}, u32[]{:S(2)}) collective-permute-start(f32[2,16,1,512]{3,2,1,0:T(1,128)S(1)} %get-tuple-element.44), channel_id=1, source_target_pairs={{0,1},{1,2},{2,3},{3,4},{4,5},{5,6},{6,7},{8,9},{9,10},{10,11},{11... | collective-permute-start | bytes 196616 | tf_op jit(solution)/shard_map/ppermute | solution.py:19
  73.6 5.6 %collective-permute-start.5 = (f32[2,16,1,512]{3,2,1,0:T(1,128)S(1)}, f32[2,16,1,512]{3,2,1,0:T(1,128)S(1)}, u32[]{:S(2)}, u32[]{:S(2)}) collective-permute-start(f32[2,16,1,512]{3,2,1,0:T(1,128)S(1)} %get-tuple-element.45), channel_id=1, source_target_pairs={{1,0},{2,1},{3,2},{4,3},{5,4},{6,5},{7,6},{9,8},{10,9},{11,10},{12... | collective-permute-start | bytes 196616 | tf_op jit(solution)/shard_map/ppermute | solution.py:20
  81.4 3.7 %copy-start.3 = (f32[1024]{0:T(1024)S(1)}, f32[1024]{0:T(1024)}, u32[]{:S(2)}) copy-start(f32[1024]{0:T(1024)} %param.15) | copy-start | bytes 12292
  81.4 3.7 %copy-start.4 = (f32[1024]{0:T(1024)S(1)}, f32[1024]{0:T(1024)}, u32[]{:S(2)}) copy-start(f32[1024]{0:T(1024)} %param.14) | copy-start | bytes 12292
  89.9 4.6 %collective-permute-start.6 = (f32[3,16,1,512]{3,2,1,0:T(1,128)S(1)}, f32[3,16,1,512]{3,2,1,0:T(1,128)S(1)}, u32[]{:S(2)}, u32[]{:S(2)}) collective-permute-start(f32[3,16,1,512]{3,2,1,0:T(1,128)S(1)} %get-tuple-element.40), channel_id=1, source_target_pairs={{0,1},{1,2},{2,3},{3,4},{4,5},{5,6},{6,7},{8,9},{9,10},{10,11},{11... | collective-permute-start | bytes 294920 | tf_op jit(solution)/shard_map/ppermute | solution.py:19
  91.8 5.9 %collective-permute-start.7 = (f32[3,16,1,512]{3,2,1,0:T(1,128)S(1)}, f32[3,16,1,512]{3,2,1,0:T(1,128)S(1)}, u32[]{:S(2)}, u32[]{:S(2)}) collective-permute-start(f32[3,16,1,512]{3,2,1,0:T(1,128)S(1)} %get-tuple-element.41), channel_id=1, source_target_pairs={{1,0},{2,1},{3,2},{4,3},{5,4},{6,5},{7,6},{9,8},{10,9},{11,10},{12... | collective-permute-start | bytes 294920 | tf_op jit(solution)/shard_map/ppermute | solution.py:20
  106.8 5.7 %collective-permute-start.8 = (f32[8,16,128]{2,1,0:T(8,128)S(1)}, f32[8,16,128]{2,1,0:T(8,128)S(1)}, u32[]{:S(2)}, u32[]{:S(2)}) collective-permute-start(f32[8,16,128]{2,1,0:T(8,128)S(1)} %bitcast.76), channel_id=1, source_target_pairs={{1,0},{2,1},{3,2},{4,3},{5,4},{6,5},{7,6},{9,8},{10,9},{11,10},{12... | collective-permute-start | bytes 196616 | tf_op jit(solution)/shard_map/ppermute | solution.py:28
  108.8 5.0 %collective-permute-start.9 = (f32[8,16,128]{2,1,0:T(8,128)S(1)}, f32[8,16,128]{2,1,0:T(8,128)S(1)}, u32[]{:S(2)}, u32[]{:S(2)}) collective-permute-start(f32[8,16,128]{2,1,0:T(8,128)S(1)} %bitcast.75), channel_id=1, source_target_pairs={{0,1},{1,2},{2,3},{3,4},{4,5},{5,6},{6,7},{8,9},{9,10},{10,11},{11... | collective-permute-start | bytes 196616 | tf_op jit(solution)/shard_map/ppermute | solution.py:28
  113.8 6.2 %collective-permute-start.10 = (f32[8,16,2,128]{3,1,0,2:T(8,128)S(1)}, f32[8,16,2,128]{3,1,0,2:T(8,128)S(1)}, u32[]{:S(2)}, u32[]{:S(2)}) collective-permute-start(f32[8,16,2,128]{3,1,0,2:T(8,128)S(1)} %get-tuple-element.67), channel_id=1, source_target_pairs={{0,1},{1,2},{2,3},{3,4},{4,5},{5,6},{6,7},{8,9},{9,10},{10,11},{11... | collective-permute-start | bytes 393224 | tf_op jit(solution)/shard_map/ppermute | solution.py:19
  118.1 6.3 %collective-permute-start.11 = (f32[8,16,2,128]{3,1,0,2:T(8,128)S(1)}, f32[8,16,2,128]{3,1,0,2:T(8,128)S(1)}, u32[]{:S(2)}, u32[]{:S(2)}) collective-permute-start(f32[8,16,2,128]{3,1,0,2:T(8,128)S(1)} %get-tuple-element.68), channel_id=1, source_target_pairs={{1,0},{2,1},{3,2},{4,3},{5,4},{6,5},{7,6},{9,8},{10,9},{11,10},{12... | collective-permute-start | bytes 393224 | tf_op jit(solution)/shard_map/ppermute | solution.py:20
